TPU v7x, 32 devices: a whole 2x2x4 slice. The times are simulated.
32 devices in a mesh: dp: 8 (over y, x, core), vocab: 4 (over z).
Axes of the slice: x: 2, y: 2, z: 4, core: 2. Of those that a mesh axis runs over, the one named last changes fastest.
Arguments:
- student_hidden: bfloat16 [1024, 1536], P('dp'), may hold values from -16 to 16
- head_weight: bfloat16 [1536, 16384], P('dp', 'vocab'), may hold values from -1 to 1
- teacher_logprobs: float32 [1024, 20480], P('dp', 'vocab'), may hold values from -45 to 0, as said below
- align_index: int32 [128, 2], replicated, may hold values from 0 to 159, as said below
- align_tiles: bfloat16 [128, 2, 128, 128], P('vocab'), may hold values from 0 to 6.1
- grad_scale: float32 [1024], P('dp'), may hold values from 30 to 300
Outputs:
- hidden_grad: bfloat16 [1024, 1536], P('dp', 'vocab')
- head_grad: bfloat16 [1536, 16384], P('dp', 'vocab')
Inputs may be any that keep to these rules, and one draw needn't show every extreme that they name: `teacher_logprobs`: each row's exponentials sum to 1 over the 20480 teacher entries. `align_index`: teacher block j is held by vocab index j // 40. Of the 64 entries of the student blocks held by one vocab index, at most 32 name teacher blocks held by any one vocab index, and for every vocab index some vocab index holds exactly 32 of them.
All inputs are finite; a program needn't handle non-finite values.
Results may differ from a plain program's by a relative error of at most 0.015.
Values may be sent and summed in bfloat16 or wider, within the bound.
No kernel may reach another device: no remote copies, remote signals or barrier semaphores. Data moves between devices by JAX's collectives and lax.ppermute only.
A program may use at most 128 MiB of HBM per device.

v0:
```python
import jax
import jax.numpy as jnp
from jax import lax
from jax.sharding import PartitionSpec as P

BLOCK = 128
K = 2


def pair_tables(index_rows, teacher_count, vocab_count):
    owner_of = index_rows // teacher_count
    local_block = index_rows % teacher_count
    onehot = (owner_of[..., None] == jnp.arange(vocab_count)[None, None, :]).astype(jnp.int32)
    running = jnp.cumsum(onehot, axis=1)
    slot_rank = jnp.sum(onehot * running, axis=2) - 1
    return (owner_of, local_block, slot_rank)


def gather_rows(x, axis):
    count = lax.axis_size(axis)
    copies = jnp.broadcast_to(x[None], (count,) + x.shape).reshape(
        (count * x.shape[0],) + x.shape[1:]
    )
    return lax.all_to_all(copies, axis, split_axis=0, concat_axis=0, tiled=True)


def scatter_hidden(partial):
    dp = lax.axis_size("dp")
    vocab = lax.axis_size("vocab")
    core = lax.axis_index("dp") % 2
    tokens, features = (partial.shape[0] // dp, partial.shape[1])
    parts = partial.astype(jnp.bfloat16).reshape(dp // 2, 2, tokens, features)
    kept = lax.dynamic_index_in_dim(parts, core, 1, keepdims=False)
    sent = lax.dynamic_index_in_dim(parts, 1 - core, 1, keepdims=False)
    got = lax.ppermute(sent, "dp", [(i, i ^ 1) for i in range(dp)])
    both = (kept.astype(jnp.float32) + got.astype(jnp.float32)).astype(jnp.bfloat16)
    groups = [[i for i in range(dp) if i % 2 == c] for c in range(2)]
    rows = lax.all_to_all(
        both, "dp", split_axis=0, concat_axis=0, axis_index_groups=groups, tiled=True
    )
    rows = jnp.sum(rows.astype(jnp.float32), axis=0).astype(jnp.bfloat16)
    last = rows.reshape(tokens, vocab, features // vocab).transpose(1, 0, 2)
    last = lax.all_to_all(last, "vocab", split_axis=0, concat_axis=0, tiled=True)
    return jnp.sum(last.astype(jnp.float32), axis=0).astype(jnp.bfloat16)


def body(student_hidden, head_weight, teacher_logprobs, align_index, align_tiles, grad_scale):
    vocab_count = lax.axis_size("vocab")
    dp_count = lax.axis_size("dp")
    own_index = lax.axis_index("vocab")
    dp_index = lax.axis_index("dp")
    tokens_here = student_hidden.shape[0]
    student_cols = head_weight.shape[1]
    student_count = student_cols // BLOCK
    teacher_count = teacher_logprobs.shape[1] // BLOCK
    pair_count = student_count * K
    capacity = (2 * pair_count + vocab_count - 1) // vocab_count
    all_rows = align_index.reshape(vocab_count, pair_count)
    owner_all, local_all, rank_all = pair_tables(all_rows, teacher_count, vocab_count)
    held_here = owner_all == own_index
    slot_numbers = jnp.arange(capacity)
    selected = (
        held_here[:, None, :] & (rank_all[:, None, :] == slot_numbers[None, :, None])
    ).astype(jnp.int32)
    source_block = jnp.sum(selected * local_all[:, None, :], axis=2).reshape(-1)
    own_owner = lax.dynamic_index_in_dim(owner_all, own_index, 0, keepdims=False)
    own_rank = lax.dynamic_index_in_dim(rank_all, own_index, 0, keepdims=False)
    where_from = own_owner * capacity + own_rank
    teacher_probs = (
        jnp.exp(teacher_logprobs)
        .astype(jnp.bfloat16)
        .reshape(tokens_here, teacher_count, BLOCK)
        .transpose(1, 0, 2)
    )
    outgoing = jnp.take(teacher_probs, source_block, axis=0)
    arrived = lax.all_to_all(outgoing, "vocab", split_axis=0, concat_axis=0, tiled=True)
    weight = lax.all_to_all(head_weight, "dp", split_axis=1, concat_axis=0, tiled=True)
    hidden = gather_rows(student_hidden, "dp")
    logits = jnp.dot(hidden, weight, preferred_element_type=jnp.float32)
    row_max = lax.pmax(jnp.max(logits, axis=1), ("dp", "vocab"))
    shifted = jnp.exp(logits - row_max[:, None])
    picked = jnp.take(arrived, where_from, axis=0).reshape(student_count, K, tokens_here, BLOCK)
    mapped_rows = jnp.einsum(
        "bktj,bkji->tbi", picked, align_tiles, preferred_element_type=jnp.float32
    )
    mapped_rows = mapped_rows.reshape(tokens_here, student_cols)
    mapped = lax.all_to_all(
        mapped_rows.astype(jnp.bfloat16), "dp", split_axis=1, concat_axis=0, tiled=True
    )
    own_rows = (jnp.arange(dp_count) == dp_index).astype(jnp.float32)[:, None]
    first = (own_index == 0).astype(jnp.float32)
    mass_part = (own_rows * jnp.sum(mapped_rows, axis=1)[None]).reshape(-1)
    scale_part = (own_rows * (first * grad_scale)[None]).reshape(-1)
    row_total, mass, scale = lax.psum(
        (jnp.sum(shifted, axis=1), mass_part, scale_part), ("dp", "vocab")
    )
    student_probs = shifted / row_total[:, None]
    dlogits = (
        scale[:, None] * (mass[:, None] * student_probs - mapped.astype(jnp.float32))
    ).astype(jnp.bfloat16)
    hidden_terms = lax.dot_general(
        dlogits, weight, (((1,), (1,)), ((), ())), preferred_element_type=jnp.float32
    )
    hidden_grad = scatter_hidden(hidden_terms)
    head_terms = lax.dot_general(
        hidden, dlogits, (((0,), (0,)), ((), ())), preferred_element_type=jnp.float32
    ).astype(jnp.bfloat16)
    head_grad = lax.all_to_all(head_terms, "dp", split_axis=0, concat_axis=1, tiled=True)
    return (hidden_grad, head_grad)


def solution(mesh):
    placed = (
        P("dp", None),
        P("dp", "vocab"),
        P("dp", "vocab"),
        P(),
        P("vocab", None, None, None),
        P("dp"),
    )
    return jax.shard_map(
        body,
        mesh=mesh,
        in_specs=placed,
        out_specs=(P("dp", "vocab"), P("dp", "vocab")),
        check_vma=False,
    )
```

profile of v0, /device:TPU:2, one launch (start us, length us, event | category | flops | bytes accessed | tf_op | source)
XLA Modules:
  0.0 344.2 jit_solution(2397335683305660772)
XLA Ops:
  0.6 2.8 copy.83
  3.5 4.4 %all-to-all-start.2 = ((bf16[192,8,512]{2,0,1:T(8,128)(2,1)}), bf16[192,8,512]{2,0,1:T(8,128)(2,1)}, u32[]{:S(2)}, u32[]{:S(2)}) async-start(bf16[192,8,512]{2,0,1:T(8,128)(2,1)} %bitcast.64), calls=%async_computation.2 | async-start | bytes 3145728 | tf_op jit(solution)/shard_map/all_to_all | solution.py:77
  7.9 0.1 copy.62
  8.1 0.1 ne.56
  8.2 0.1 copy.64
  8.8 3.2 copy.65
  12.0 3.2 exponential_convert_fusion
  15.2 0.1 reduce_window_sum.11
  15.3 0.2 select_reduce_fusion
  15.5 0.1 select_reduce_fusion.1
  15.9 1.8 copy.66
  17.7 3.1 gather_fusion
  20.7 4.6 %broadcast_select_fusion = bf16[128,128,128]{2,1,0:T(8,128)(2,1)} fusion(bf16[128,128,128]{2,1,0:T(8,128)(2,1)} %gather_fusion, pred[128]{0:T(512)(128)(4,1)S(1)} %compare_and_fusion.1), kind=kLoop, calls=%fused_computation.2 | loop fusion | flops 2097152 | bytes 8388736 | tf_op jit(solution)/shard_map/jit(_take)/select_n | solution.py:75
  25.3 2.1 all-to-all-done.2
  27.5 99.8 %all_to_all.72 = bf16[128,128,128]{2,1,0:T(8,128)(2,1)} all-to-all(bf16[128,128,128]{2,1,0:T(8,128)(2,1)} %broadcast_select_fusion), channel_id=1, replica_groups=mesh['dp'=8,'vocab'=4] {'vocab'}, dimensions={0} | all-to-all | bytes 8388608 | tf_op jit(solution)/shard_map/all_to_all | solution.py:76
  127.3 2.0 broadcast_in_dim.26
  129.3 4.5 %all-to-all-start.1 = ((bf16[8,128,1536]{2,1,0:T(8,128)(2,1)}), bf16[8,128,1536]{2,1,0:T(8,128)(2,1)}, u32[]{:S(2)}, u32[]{:S(2)}) async-start(bf16[8,128,1536]{2,1,0:T(8,128)(2,1)} %broadcast_in_dim.26), calls=%async_computation.1 | async-start | bytes 6291456 | tf_op jit(solution)/shard_map/all_to_all | solution.py:24
  133.8 0.5 broadcast.181
  134.3 0.7 fusion.16
  135.2 4.3 %gather_fusion.1 = bf16[64,128,128]{2,1,0:T(8,128)(2,1)} fusion(bf16[128,128,128]{2,1,0:T(8,128)(2,1)} %all_to_all.72, s32[1024]{0:T(1024)S(1)} %pad_clamp_fusion), kind=kCustom, calls=%fused_computation.1 | custom fusion | bytes 4194560 | tf_op jit(solution)/shard_map/jit(_take)/gather | solution.py:82
  139.5 4.1 %bitcast_convert_fusion = (bf16[32,128,128]{1,2,0:T(8,128)(2,1)}, f32[32,128,128,1]{1,2,3,0:T(8,128)}) fusion(bf16[32,2,128,128]{3,2,1,0:T(8,128)(2,1)S(1)} %copy-done, bf16[32,2,128,128]{3,2,1,0:T(8,128)(2,1)} %bitcast.63, pred[32,2]{1,0:T(8,128)(4,1)S(1)} %compare_and_fusion), kind=kOutput, calls=%fused_computation.12 | convolution fusion | flops 270008320 | bytes 7340096 | tf_op jit(solution)/shard_map/bktj,bkji->tbi/dot_general | solution.py:83
  143.6 25.5 %all-to-all-done.1 = bf16[8,128,1536]{2,1,0:T(8,128)(2,1)} async-done(((bf16[8,128,1536]{2,1,0:T(8,128)(2,1)}), bf16[8,128,1536]{2,1,0:T(8,128)(2,1)}, u32[]{:S(2)}, u32[]{:S(2)}) %all-to-all-start.1) | async-done | bytes 3145760 | tf_op jit(solution)/shard_map/all_to_all | solution.py:24
  169.1 5.0 %all-to-all-start.3 = ((bf16[128,8,512]{0,2,1:T(8,128)(2,1)}), bf16[128,8,512]{0,2,1:T(8,128)(2,1)S(1)}, u32[]{:S(2)}, u32[]{:S(2)}) async-start(bf16[128,8,512]{0,2,1:T(8,128)(2,1)} %bitcast.14), calls=%async_computation.3 | async-start | bytes 2097152 | tf_op jit(solution)/shard_map/all_to_all | solution.py:87
  174.1 5.5 %fusion.18 = (f32[1024]{0:T(1024)S(1)}, f32[1024,512]{0,1:T(8,128)}) fusion(bf16[1024,1536]{1,0:T(8,128)(2,1)} %bitcast.10, bf16[1536,512]{1,0:T(8,128)(2,1)} %bitcast.12), kind=kOutput, calls=%fused_computation.57 | convolution fusion | flops 1611136000 | bytes 6819840 | tf_op jit(solution)/shard_map/dot_general | solution.py:79
  179.6 41.5 %pmax.7 = f32[1024]{0:T(1024)S(1)} all-reduce(f32[1024]{0:T(1024)S(1)} %get-tuple-element.15), channel_id=1, replica_groups=mesh['dp'=8,'vocab'=4] {'dp','vocab'}, use_global_device_ids=true, to_apply=%region_7.8 | all-reduce | flops 1024 | bytes 8192 | tf_op jit(solution)/shard_map/pmax | solution.py:80
  221.1 2.1 fusion.7
  223.2 0.2 copy-done.1
  223.3 0.6 bitcast_reduce_fusion
  223.9 39.5 %all-reduce = (f32[1024]{0:T(1024)S(1)}, f32[1024]{0:T(1024)S(1)}, f32[1024]{0:T(1024)S(1)}) all-reduce(f32[1024]{0:T(1024)S(1)} %fusion.7, f32[1024]{0:T(1024)S(1)} %get-tuple-element.12, f32[1024]{0:T(1024)S(1)} %get-tuple-element.11), channel_id=1, replica_groups=mesh['dp'=8,'vocab'=4] {'dp','vocab'}, use_global_device_ids=true, to_apply=%region_9.10 | all-reduce | flops 3072 | bytes 24576 | tf_op jit(solution)/shard_map/psum | solution.py:94
  263.4 2.2 fusion.3
  265.6 3.6 %convolution_convert_fusion = bf16[1024,1536]{1,0:T(8,128)(2,1)S(1)} fusion(bf16[1024,512]{0,1:T(8,128)(2,1)S(1)} %fusion.3, bf16[1536,512]{1,0:T(8,128)(2,1)} %bitcast.12), kind=kOutput, calls=%fused_computation.3 | convolution fusion | flops 1612185600 | bytes 5767168 | tf_op jit(solution)/shard_map/dot_general | solution.py:101
  269.3 1.7 copy-done.2
  271.0 1.2 dynamic-slice_bitcast_fusion
  272.2 3.7 %collective-permute-done = bf16[4,128,1536]{2,1,0:T(8,128)(2,1)} collective-permute-done((bf16[4,128,1536]{2,1,0:T(8,128)(2,1)}, bf16[4,128,1536]{2,1,0:T(8,128)(2,1)}, u32[]{:S(2)}, u32[]{:S(2)}) %collective-permute-start) | collective-permute-done | bytes 1572896 | tf_op jit(solution)/shard_map/ppermute | solution.py:35
  276.0 3.4 fusion
  279.4 4.5 %all-to-all-start.4 = ((bf16[4,128,1536]{2,1,0:T(8,128)(2,1)}), bf16[4,128,1536]{2,1,0:T(8,128)(2,1)}, u32[]{:S(2)}, u32[]{:S(2)}) async-start(bf16[4,128,1536]{2,1,0:T(8,128)(2,1)} %fusion), calls=%async_computation.4 | async-start | bytes 3145728 | tf_op jit(solution)/shard_map/all_to_all | solution.py:38
  283.9 4.9 %fusion.1 = bf16[1536,512]{0,1:T(8,128)(2,1)} fusion(bf16[1024,512]{0,1:T(8,128)(2,1)S(1)} %copy-done.4, bf16[1024,1536]{1,0:T(8,128)(2,1)} %bitcast.10), kind=kOutput, calls=%fused_computation.7 | convolution fusion | flops 1611399168 | bytes 5767168 | tf_op jit(solution)/shard_map/dot_general | solution.py:105
  288.8 2.6 copy.73
  291.4 12.1 %all-to-all-done.4 = bf16[4,128,1536]{2,1,0:T(8,128)(2,1)} async-done(((bf16[4,128,1536]{2,1,0:T(8,128)(2,1)}), bf16[4,128,1536]{2,1,0:T(8,128)(2,1)}, u32[]{:S(2)}, u32[]{:S(2)}) %all-to-all-start.4) | async-done | bytes 1572896 | tf_op jit(solution)/shard_map/all_to_all | solution.py:38
  303.5 4.8 %all-to-all-start.6 = ((bf16[8,192,512]{2,1,0:T(8,128)(2,1)}), bf16[8,192,512]{2,1,0:T(8,128)(2,1)}, u32[]{:S(2)}, u32[]{:S(2)}) async-start(bf16[8,192,512]{2,1,0:T(8,128)(2,1)} %bitcast.65), calls=%async_computation.6 | async-start | bytes 3145728 | tf_op jit(solution)/shard_map/all_to_all | solution.py:108
  308.2 1.7 reduce_sum.64
  309.9 0.2 copy.71
  310.1 0.9 copy.72
  311.0 16.8 %all-to-all-done.6 = bf16[8,192,512]{2,1,0:T(8,128)(2,1)} async-done(((bf16[8,192,512]{2,1,0:T(8,128)(2,1)}), bf16[8,192,512]{2,1,0:T(8,128)(2,1)}, u32[]{:S(2)}, u32[]{:S(2)}) %all-to-all-start.6) | async-done | bytes 1572896 | tf_op jit(solution)/shard_map/all_to_all | solution.py:108
  327.8 3.5 %all-to-all-start.5 = ((bf16[4,128,384]{2,1,0:T(8,128)(2,1)}), bf16[4,128,384]{2,1,0:T(8,128)(2,1)S(1)}, u32[]{:S(2)}, u32[]{:S(2)}) async-start(bf16[4,128,384]{2,1,0:T(8,128)(2,1)} %copy.72), calls=%async_computation.5 | async-start | bytes 786432 | tf_op jit(solution)/shard_map/all_to_all | solution.py:43
  331.3 2.7 copy.80
  334.1 9.4 %all-to-all-done.5 = bf16[4,128,384]{2,1,0:T(8,128)(2,1)S(1)} async-done(((bf16[4,128,384]{2,1,0:T(8,128)(2,1)}), bf16[4,128,384]{2,1,0:T(8,128)(2,1)S(1)}, u32[]{:S(2)}, u32[]{:S(2)}) %all-to-all-start.5) | async-done | bytes 393248 | tf_op jit(solution)/shard_map/all_to_all | solution.py:43
  343.5 0.7 reduce_sum.65
  (36 shorter events, 0.9 us)
Async XLA Ops:
  0.6 138.9 %copy-start = (bf16[32,2,128,128]{3,2,1,0:T(8,128)(2,1)S(1)}, bf16[32,2,128,128]{3,2,1,0:T(8,128)(2,1)}, u32[]{:S(2)}) copy-start(bf16[32,2,128,128]{3,2,1,0:T(8,128)(2,1)} %param.10) | copy-start | bytes 6291460
  3.5 4.4 %copy-start.6 = (s32[128,2]{0,1:T(2,128)S(1)}, s32[128,2]{0,1:T(2,128)}, u32[]{:S(2)}) copy-start(s32[128,2]{0,1:T(2,128)} %param.9) | copy-start | bytes 3076
  3.5 24.0 %all-to-all-start.2 = ((bf16[192,8,512]{2,0,1:T(8,128)(2,1)}), bf16[192,8,512]{2,0,1:T(8,128)(2,1)}, u32[]{:S(2)}, u32[]{:S(2)}) async-start(bf16[192,8,512]{2,0,1:T(8,128)(2,1)} %bitcast.64), calls=%async_computation.2 | async-start | bytes 3145728 | tf_op jit(solution)/shard_map/all_to_all | solution.py:77
  25.3 101.9 %copy-start.5 = (bf16[128,1536]{1,0:T(8,128)(2,1)S(1)}, bf16[128,1536]{1,0:T(8,128)(2,1)}, u32[]{:S(2)}) copy-start(bf16[128,1536]{1,0:T(8,128)(2,1)} %param.6) | copy-start | bytes 1179652
  129.2 5.9 %copy-start.7 = (f32[128]{0:T(128)S(1)}, f32[128]{0:T(128)}, u32[]{:S(2)}) copy-start(f32[128]{0:T(128)} %param.11) | copy-start | bytes 1540
  129.3 39.9 %all-to-all-start.1 = ((bf16[8,128,1536]{2,1,0:T(8,128)(2,1)}), bf16[8,128,1536]{2,1,0:T(8,128)(2,1)}, u32[]{:S(2)}, u32[]{:S(2)}) async-start(bf16[8,128,1536]{2,1,0:T(8,128)(2,1)} %broadcast_in_dim.26), calls=%async_computation.1 | async-start | bytes 6291456 | tf_op jit(solution)/shard_map/all_to_all | solution.py:24
  169.1 94.3 %all-to-all-start.3 = ((bf16[128,8,512]{0,2,1:T(8,128)(2,1)}), bf16[128,8,512]{0,2,1:T(8,128)(2,1)S(1)}, u32[]{:S(2)}, u32[]{:S(2)}) async-start(bf16[128,8,512]{0,2,1:T(8,128)(2,1)} %bitcast.14), calls=%async_computation.3 | async-start | bytes 2097152 | tf_op jit(solution)/shard_map/all_to_all | solution.py:87
  221.1 2.2 copy-start.1
  265.6 3.7 %copy-start.3 = (bf16[1024,512]{0,1:T(8,128)(2,1)}, bf16[1024,512]{0,1:T(8,128)(2,1)S(1)}, u32[]{:S(2)}) copy-start(bf16[1024,512]{0,1:T(8,128)(2,1)S(1)} %fusion.3) | copy-start | bytes 3145732
  269.3 1.7 copy-start.2
  272.2 3.8 %collective-permute-start = (bf16[4,128,1536]{2,1,0:T(8,128)(2,1)}, bf16[4,128,1536]{2,1,0:T(8,128)(2,1)}, u32[]{:S(2)}, u32[]{:S(2)}) collective-permute-start(bf16[4,128,1536]{2,1,0:T(8,128)(2,1)} %dynamic-slice_bitcast_fusion), channel_id=1, source_target_pairs={{0,4},{4,0},{8,12},{12,8},{16,20},{20,16},{24,28},{28,24},{1,5},{5... | collective-permute-start | bytes 4718600 | tf_op jit(solution)/shard_map/ppermute | solution.py:35
  279.4 4.5 %copy-start.4 = (bf16[1024,512]{0,1:T(8,128)(2,1)S(1)}, bf16[1024,512]{0,1:T(8,128)(2,1)}, u32[]{:S(2)}) copy-start(bf16[1024,512]{0,1:T(8,128)(2,1)} %copy-done.3) | copy-start | bytes 3145732
  279.4 24.1 %all-to-all-start.4 = ((bf16[4,128,1536]{2,1,0:T(8,128)(2,1)}), bf16[4,128,1536]{2,1,0:T(8,128)(2,1)}, u32[]{:S(2)}, u32[]{:S(2)}) async-start(bf16[4,128,1536]{2,1,0:T(8,128)(2,1)} %fusion), calls=%async_computation.4 | async-start | bytes 3145728 | tf_op jit(solution)/shard_map/all_to_all | solution.py:38
  303.5 24.4 %all-to-all-start.6 = ((bf16[8,192,512]{2,1,0:T(8,128)(2,1)}), bf16[8,192,512]{2,1,0:T(8,128)(2,1)}, u32[]{:S(2)}, u32[]{:S(2)}) async-start(bf16[8,192,512]{2,1,0:T(8,128)(2,1)} %bitcast.65), calls=%async_computation.6 | async-start | bytes 3145728 | tf_op jit(solution)/shard_map/all_to_all | solution.py:108
  327.8 15.6 %all-to-all-start.5 = ((bf16[4,128,384]{2,1,0:T(8,128)(2,1)}), bf16[4,128,384]{2,1,0:T(8,128)(2,1)S(1)}, u32[]{:S(2)}, u32[]{:S(2)}) async-start(bf16[4,128,384]{2,1,0:T(8,128)(2,1)} %copy.72), calls=%async_computation.5 | async-start | bytes 786432 | tf_op jit(solution)/shard_map/all_to_all | solution.py:43
where the time goes:
time: 345 us; the launch traced here: 344 us
  blocking collectives  181 us (52%)
  waiting for transfers between devices  69.7 us (20%)
  local copies, waits for them, and re-layouts  28.3 us (8%)
  starting transfers between devices  26.6 us (8%)
  other arithmetic  19.8 us (6%)
  matrix products  18.1 us (5%)
    all_to_all x1, blocking collectives, body(): lax.all_to_all(outgoing, 'vocab', split_axis=0, concat_axis=0, tiled=True)  99.8 us
    pmax x1, blocking collectives, body(): row_max = lax.pmax(jnp.max(logits, axis=1), ('dp', 'vocab'))  41.5 us
    psum x1, blocking collectives, body(): lax.psum((jnp.sum(shifted, axis=1), mass_part, scale_part), ('dp', 'vocab'))  39.5 us
    all_to_all x1, waiting for transfers between devices, gather_rows(): return lax.all_to_all(copies, axis, split_axis=0, concat_axis=0, tiled=True)  25.5 us
    all_to_all x1, waiting for transfers between devices, body(): lax.all_to_all(head_terms, 'dp', split_axis=0, concat_axis=1, tiled=True)  16.8 us
    all_to_all x1, waiting for transfers between devices, scatter_hidden(): lax.all_to_all(both, 'dp', split_axis=0, concat_axis=0, axis_index_groups...  12.1 us
    all_to_all x1, waiting for transfers between devices, scatter_hidden(): lax.all_to_all(last, 'vocab', split_axis=0, concat_axis=0, tiled=True)  9.4 us
  transfers between devices with their start and end apart: 7, of which 6 were waited for; matrix products, arithmetic and copies ran while one was open for 14% of the time, Pallas kernels for 0%

commit v1 on v0

--- a/solution.py
+++ b/solution.py
@@ -5,6 +5,22 @@
 
 BLOCK = 128
 K = 2
+
+
+def swapped_with_each(x, axis, split, join):
+    ways, here = (lax.axis_size(axis), lax.axis_index(axis))
+    width = x.shape[split] // ways
+    lengths = list(x.shape)
+    lengths[split] = width
+    height = lengths[join]
+    lengths[join] = height * ways
+    full = jnp.zeros(lengths, x.dtype)
+    for mask in range(ways):
+        part = lax.dynamic_slice_in_dim(x, (here ^ mask) * width, width, axis=split)
+        if mask:
+            part = lax.ppermute(part, axis, [(d, d ^ mask) for d in range(ways)])
+        full = lax.dynamic_update_slice_in_dim(full, part, (here ^ mask) * height, axis=join)
+    return full
 
 
 def pair_tables(index_rows, teacher_count, vocab_count):
@@ -105,7 +121,7 @@
     head_terms = lax.dot_general(
         hidden, dlogits, (((0,), (0,)), ((), ())), preferred_element_type=jnp.float32
     ).astype(jnp.bfloat16)
-    head_grad = lax.all_to_all(head_terms, "dp", split_axis=0, concat_axis=1, tiled=True)
+    head_grad = swapped_with_each(head_terms, "dp", 0, 1)
     return (hidden_grad, head_grad)
 
 

time: 345 us -> 334 us (0.968)
  waiting for transfers between devices: 69.7 us -> 44.7 us
  local copies, waits for them, and re-layouts: 28.3 us -> 39.4 us
    all_to_all x1 -> x0, waiting for transfers between devices: 16.8 us -> none  [body(): lax.all_to_all(head_terms, 'dp', split_axis=0, concat_axis=1, tiled=True)]
    ppermute x0 -> x7, waiting for transfers between devices: none -> 13.3 us  [swapped_with_each(): part = lax.ppermute(part, axis, [(d, d ^ mask) for d in range(ways)])]
    all_to_all x1, waiting for transfers between devices: 12.1 us -> 0.01 us  [scatter_hidden(): lax.all_to_all(both, 'dp', split_axis=0, concat_axis=0, axis_index_groups...]
    all_to_all x1, waiting for transfers between devices: 9.4 us -> 0.01 us  [scatter_hidden(): lax.all_to_all(last, 'vocab', split_axis=0, concat_axis=0, tiled=True)]
    ppermute x0 -> x7, local copies, waits for them, and re-layouts: none -> 7.51 us  [swapped_with_each(): part = lax.ppermute(part, axis, [(d, d ^ mask) for d in range(ways)])]
    ppermute x0 -> x7, starting transfers between devices: none -> 6.36 us  [swapped_with_each(): part = lax.ppermute(part, axis, [(d, d ^ mask) for d in range(ways)])]
    dynamic_update_slice x0 -> x8, local copies, waits for them, and re-layouts: none -> 5.53 us  [swapped_with_each(): lax.dynamic_update_slice_in_dim(full, part, (here ^ mask) * height, axis=...]
    all_to_all x1 -> x0, starting transfers between devices: 4.77 us -> none  [body(): lax.all_to_all(head_terms, 'dp', split_axis=0, concat_axis=1, tiled=True)]
  transfers between devices with their start and end apart: 7 -> 13, of which waited for: 6 -> 5; matrix products, arithmetic and copies ran while one was open for 14% -> 18% of each run, Pallas kernels for 0% -> 0%
where the time goes in v1:
time: 334 us; the launch traced here: 331 us
  blocking collectives  181 us (54%)
  waiting for transfers between devices  44.7 us (13%)
  local copies, waits for them, and re-layouts  39.4 us (12%)
  starting transfers between devices  28.8 us (9%)
  other arithmetic  19.9 us (6%)
  matrix products  16.9 us (5%)
    all_to_all x1, blocking collectives, body(): lax.all_to_all(outgoing, 'vocab', split_axis=0, concat_axis=0, tiled=True)  99.8 us
    pmax x1, blocking collectives, body(): row_max = lax.pmax(jnp.max(logits, axis=1), ('dp', 'vocab'))  41.5 us
    psum x1, blocking collectives, body(): lax.psum((jnp.sum(shifted, axis=1), mass_part, scale_part), ('dp', 'vocab'))  39.5 us
    all_to_all x1, waiting for transfers between devices, gather_rows(): return lax.all_to_all(copies, axis, split_axis=0, concat_axis=0, tiled=True)  25.5 us
    ppermute x7, waiting for transfers between devices, swapped_with_each(): part = lax.ppermute(part, axis, [(d, d ^ mask) for d in range(ways)])  13.3 us
    ppermute x7, local copies, waits for them, and re-layouts, swapped_with_each(): part = lax.ppermute(part, axis, [(d, d ^ mask) for d in range(ways)])  7.51 us
  transfers between devices with their start and end apart: 13, of which 5 were waited for; matrix products, arithmetic and copies ran while one was open for 18% of the time, Pallas kernels for 0%

profile of v1, /device:TPU:2, one launch (start us, length us, event | category | flops | bytes accessed | tf_op | source)
XLA Modules:
  0.0 331.5 jit_solution(17894899028369791902)
XLA Ops:
  0.6 2.8 copy.126
  3.5 4.4 %all-to-all-start.2 = ((bf16[192,8,512]{2,0,1:T(8,128)(2,1)}), bf16[192,8,512]{2,0,1:T(8,128)(2,1)}, u32[]{:S(2)}, u32[]{:S(2)}) async-start(bf16[192,8,512]{2,0,1:T(8,128)(2,1)} %bitcast.74), calls=%async_computation.2 | async-start | bytes 3145728 | tf_op jit(solution)/shard_map/all_to_all | solution.py:93
  8.8 3.2 copy.103
  12.0 3.2 exponential_convert_fusion
  15.9 1.8 copy.104
  17.7 3.1 gather_fusion
  20.7 4.6 %broadcast_select_fusion = bf16[128,128,128]{2,1,0:T(8,128)(2,1)} fusion(bf16[128,128,128]{2,1,0:T(8,128)(2,1)} %gather_fusion, pred[128]{0:T(512)(128)(4,1)S(1)} %compare_and_fusion.1), kind=kLoop, calls=%fused_computation.2 | loop fusion | flops 2097152 | bytes 8388736 | tf_op jit(solution)/shard_map/jit(_take)/select_n | solution.py:91
  25.4 2.1 all-to-all-done.2
  27.5 99.8 %all_to_all.53 = bf16[128,128,128]{2,1,0:T(8,128)(2,1)} all-to-all(bf16[128,128,128]{2,1,0:T(8,128)(2,1)} %broadcast_select_fusion), channel_id=1, replica_groups=mesh['dp'=8,'vocab'=4] {'vocab'}, dimensions={0} | all-to-all | bytes 8388608 | tf_op jit(solution)/shard_map/all_to_all | solution.py:92
  127.3 2.0 broadcast_in_dim.28
  129.2 4.5 %all-to-all-start.1 = ((bf16[8,128,1536]{2,1,0:T(8,128)(2,1)}), bf16[8,128,1536]{2,1,0:T(8,128)(2,1)}, u32[]{:S(2)}, u32[]{:S(2)}) async-start(bf16[8,128,1536]{2,1,0:T(8,128)(2,1)} %broadcast_in_dim.28), calls=%async_computation.1 | async-start | bytes 6291456 | tf_op jit(solution)/shard_map/all_to_all | solution.py:40
  135.2 4.3 %gather_fusion.1 = bf16[64,128,128]{2,1,0:T(8,128)(2,1)} fusion(bf16[128,128,128]{2,1,0:T(8,128)(2,1)} %all_to_all.53, s32[1024]{0:T(1024)S(1)} %pad_clamp_fusion), kind=kCustom, calls=%fused_computation.1 | custom fusion | bytes 4194560 | tf_op jit(solution)/shard_map/jit(_take)/gather | solution.py:98
  139.5 4.1 %bitcast_convert_fusion = (bf16[32,128,128]{1,2,0:T(8,128)(2,1)}, f32[32,128,128,1]{1,2,3,0:T(8,128)}) fusion(bf16[32,2,128,128]{3,2,1,0:T(8,128)(2,1)S(1)} %copy-done, bf16[32,2,128,128]{3,2,1,0:T(8,128)(2,1)} %bitcast.73, pred[32,2]{1,0:T(8,128)(4,1)S(1)} %compare_and_fusion), kind=kOutput, calls=%fused_computation.11 | convolution fusion | flops 270008320 | bytes 7340096 | tf_op jit(solution)/shard_map/bktj,bkji->tbi/dot_general | solution.py:99
  143.6 25.5 %all-to-all-done.1 = bf16[8,128,1536]{2,1,0:T(8,128)(2,1)} async-done(((bf16[8,128,1536]{2,1,0:T(8,128)(2,1)}), bf16[8,128,1536]{2,1,0:T(8,128)(2,1)}, u32[]{:S(2)}, u32[]{:S(2)}) %all-to-all-start.1) | async-done | bytes 3145760 | tf_op jit(solution)/shard_map/all_to_all | solution.py:40
  169.1 5.0 %all-to-all-start.3 = ((bf16[128,8,512]{0,2,1:T(8,128)(2,1)}), bf16[128,8,512]{0,2,1:T(8,128)(2,1)S(1)}, u32[]{:S(2)}, u32[]{:S(2)}) async-start(bf16[128,8,512]{0,2,1:T(8,128)(2,1)} %bitcast.14), calls=%async_computation.3 | async-start | bytes 2097152 | tf_op jit(solution)/shard_map/all_to_all | solution.py:103
  174.1 5.5 %fusion.17 = (f32[1024]{0:T(1024)S(1)}, f32[1024,512]{0,1:T(8,128)}) fusion(bf16[1024,1536]{1,0:T(8,128)(2,1)} %bitcast.10, bf16[1536,512]{1,0:T(8,128)(2,1)} %bitcast.12), kind=kOutput, calls=%fused_computation.72 | convolution fusion | flops 1611136000 | bytes 6819840 | tf_op jit(solution)/shard_map/dot_general | solution.py:95
  179.6 41.5 %pmax.7 = f32[1024]{0:T(1024)S(1)} all-reduce(f32[1024]{0:T(1024)S(1)} %get-tuple-element.23), channel_id=1, replica_groups=mesh['dp'=8,'vocab'=4] {'dp','vocab'}, use_global_device_ids=true, to_apply=%region_7.8 | all-reduce | flops 1024 | bytes 8192 | tf_op jit(solution)/shard_map/pmax | solution.py:96
  221.1 2.1 fusion.6
  223.9 39.5 %all-reduce = (f32[1024]{0:T(1024)S(1)}, f32[1024]{0:T(1024)S(1)}, f32[1024]{0:T(1024)S(1)}) all-reduce(f32[1024]{0:T(1024)S(1)} %fusion.6, f32[1024]{0:T(1024)S(1)} %get-tuple-element.20, f32[1024]{0:T(1024)S(1)} %get-tuple-element.19), channel_id=1, replica_groups=mesh['dp'=8,'vocab'=4] {'dp','vocab'}, use_global_device_ids=true, to_apply=%region_9.10 | all-reduce | flops 3072 | bytes 24576 | tf_op jit(solution)/shard_map/psum | solution.py:110
  263.4 2.2 fusion.2
  265.6 3.6 %convolution_convert_fusion = bf16[1024,1536]{1,0:T(8,128)(2,1)S(1)} fusion(bf16[1024,512]{0,1:T(8,128)(2,1)S(1)} %fusion.2, bf16[1536,512]{1,0:T(8,128)(2,1)} %bitcast.12), kind=kOutput, calls=%fused_computation.3 | convolution fusion | flops 1612185600 | bytes 5767168 | tf_op jit(solution)/shard_map/dot_general | solution.py:117
  269.3 1.6 copy-done.2
  270.9 1.2 dynamic-slice_bitcast_fusion
  272.2 3.7 %collective-permute-done = bf16[4,128,1536]{2,1,0:T(8,128)(2,1)} collective-permute-done((bf16[4,128,1536]{2,1,0:T(8,128)(2,1)}, bf16[4,128,1536]{2,1,0:T(8,128)(2,1)}, u32[]{:S(2)}, u32[]{:S(2)}) %collective-permute-start) | collective-permute-done | bytes 1572896 | tf_op jit(solution)/shard_map/ppermute | solution.py:51
  275.9 3.5 %fusion = bf16[4,128,1536]{2,1,0:T(8,128)(2,1)} fusion(bf16[4,128,1536]{2,1,0:T(8,128)(2,1)} %collective-permute-done, bf16[4,2,128,1536]{3,2,1,0:T(8,128)(2,1)} %bitcast.77, s32[]{:T(128)S(6)} %select_n.142), kind=kLoop, calls=%fused_computation.5 | loop fusion | flops 3145728 | bytes 4718596 | tf_op jit(solution)/shard_map/convert_element_type | solution.py:52
  279.4 4.5 %all-to-all-start.4 = ((bf16[4,128,1536]{2,1,0:T(8,128)(2,1)}), bf16[4,128,1536]{2,1,0:T(8,128)(2,1)}, u32[]{:S(2)}, u32[]{:S(2)}) async-start(bf16[4,128,1536]{2,1,0:T(8,128)(2,1)} %fusion), calls=%async_computation.4 | async-start | bytes 3145728 | tf_op jit(solution)/shard_map/all_to_all | solution.py:54
  284.0 3.7 %convolution_convert_fusion.1 = bf16[512,1536]{1,0:T(8,128)(2,1)S(1)} fusion(bf16[1024,512]{0,1:T(8,128)(2,1)S(1)} %copy-done.4, bf16[1024,1536]{1,0:T(8,128)(2,1)} %bitcast.10), kind=kOutput, calls=%fused_computation.6 | convolution fusion | flops 1611399168 | bytes 5767168 | tf_op jit(solution)/shard_map/dot_general | solution.py:121
  287.6 2.0 dynamic-slice_bitcast_fusion.1
  289.9 1.8 collective-permute-start.3
  291.7 1.1 collective-permute-start.4
  293.5 1.3 broadcast_in_dim.29
  295.5 1.5 collective-permute-start.6
  297.0 1.1 copy.112
  298.1 10.0 %collective-permute-done.2 = bf16[192,512]{0,1:T(8,128)(2,1)} collective-permute-done((bf16[192,512]{0,1:T(8,128)(2,1)S(1)}, bf16[192,512]{0,1:T(8,128)(2,1)}, u32[]{:S(2)}, u32[]{:S(2)}) %collective-permute-start.2) | collective-permute-done | bytes 196640 | tf_op jit(solution)/shard_map/ppermute | solution.py:21
  308.0 1.2 collective-permute-start.7
  309.2 1.1 copy.113
  310.3 0.7 constant_dynamic-update-slice_fusion.5
  311.0 1.7 reduce_sum.64
  312.9 0.9 copy.110
  313.8 4.1 %all-to-all-start.5 = ((bf16[4,128,384]{2,1,0:T(8,128)(2,1)}), bf16[4,128,384]{2,1,0:T(8,128)(2,1)S(1)}, u32[]{:S(2)}, u32[]{:S(2)}) async-start(bf16[4,128,384]{2,1,0:T(8,128)(2,1)} %copy.110), calls=%async_computation.5 | async-start | bytes 786432 | tf_op jit(solution)/shard_map/all_to_all | solution.py:59
  318.6 1.1 copy.114
  319.7 1.1 copy.115
  320.8 3.3 collective-permute-done.5
  324.1 1.1 copy.116
  325.2 1.1 copy.117
  326.2 1.1 copy.118
  327.3 0.7 constant_dynamic-update-slice_fusion.3
  330.8 0.7 reduce_sum.65
  (64 shorter events, 8.9 us)
Async XLA Ops:
  0.6 138.8 %copy-start = (bf16[32,2,128,128]{3,2,1,0:T(8,128)(2,1)S(1)}, bf16[32,2,128,128]{3,2,1,0:T(8,128)(2,1)}, u32[]{:S(2)}) copy-start(bf16[32,2,128,128]{3,2,1,0:T(8,128)(2,1)} %param.10) | copy-start | bytes 6291460
  3.5 4.4 %copy-start.6 = (s32[128,2]{0,1:T(2,128)S(1)}, s32[128,2]{0,1:T(2,128)}, u32[]{:S(2)}) copy-start(s32[128,2]{0,1:T(2,128)} %param.9) | copy-start | bytes 3076
  3.5 24.0 %all-to-all-start.2 = ((bf16[192,8,512]{2,0,1:T(8,128)(2,1)}), bf16[192,8,512]{2,0,1:T(8,128)(2,1)}, u32[]{:S(2)}, u32[]{:S(2)}) async-start(bf16[192,8,512]{2,0,1:T(8,128)(2,1)} %bitcast.74), calls=%async_computation.2 | async-start | bytes 3145728 | tf_op jit(solution)/shard_map/all_to_all | solution.py:93
  25.4 101.9 %copy-start.5 = (bf16[128,1536]{1,0:T(8,128)(2,1)S(1)}, bf16[128,1536]{1,0:T(8,128)(2,1)}, u32[]{:S(2)}) copy-start(bf16[128,1536]{1,0:T(8,128)(2,1)} %param.6) | copy-start | bytes 1179652
  129.2 5.9 %copy-start.7 = (f32[128]{0:T(128)S(1)}, f32[128]{0:T(128)}, u32[]{:S(2)}) copy-start(f32[128]{0:T(128)} %param.11) | copy-start | bytes 1540
  129.2 39.9 %all-to-all-start.1 = ((bf16[8,128,1536]{2,1,0:T(8,128)(2,1)}), bf16[8,128,1536]{2,1,0:T(8,128)(2,1)}, u32[]{:S(2)}, u32[]{:S(2)}) async-start(bf16[8,128,1536]{2,1,0:T(8,128)(2,1)} %broadcast_in_dim.28), calls=%async_computation.1 | async-start | bytes 6291456 | tf_op jit(solution)/shard_map/all_to_all | solution.py:40
  169.1 94.3 %all-to-all-start.3 = ((bf16[128,8,512]{0,2,1:T(8,128)(2,1)}), bf16[128,8,512]{0,2,1:T(8,128)(2,1)S(1)}, u32[]{:S(2)}, u32[]{:S(2)}) async-start(bf16[128,8,512]{0,2,1:T(8,128)(2,1)} %bitcast.14), calls=%async_computation.3 | async-start | bytes 2097152 | tf_op jit(solution)/shard_map/all_to_all | solution.py:103
  221.1 2.2 copy-start.1
  265.6 3.7 %copy-start.3 = (bf16[1024,512]{0,1:T(8,128)(2,1)}, bf16[1024,512]{0,1:T(8,128)(2,1)S(1)}, u32[]{:S(2)}) copy-start(bf16[1024,512]{0,1:T(8,128)(2,1)S(1)} %fusion.2) | copy-start | bytes 3145732
  269.3 1.7 copy-start.2
  272.2 3.8 %collective-permute-start = (bf16[4,128,1536]{2,1,0:T(8,128)(2,1)}, bf16[4,128,1536]{2,1,0:T(8,128)(2,1)}, u32[]{:S(2)}, u32[]{:S(2)}) collective-permute-start(bf16[4,128,1536]{2,1,0:T(8,128)(2,1)} %dynamic-slice_bitcast_fusion), channel_id=1, source_target_pairs={{0,4},{4,0},{8,12},{12,8},{16,20},{20,16},{24,28},{28,24},{1,5},{5... | collective-permute-start | bytes 4718600 | tf_op jit(solution)/shard_map/ppermute | solution.py:51
  279.4 4.5 %copy-start.4 = (bf16[1024,512]{0,1:T(8,128)(2,1)S(1)}, bf16[1024,512]{0,1:T(8,128)(2,1)}, u32[]{:S(2)}) copy-start(bf16[1024,512]{0,1:T(8,128)(2,1)} %copy-done.3) | copy-start | bytes 3145732
  279.4 31.5 %all-to-all-start.4 = ((bf16[4,128,1536]{2,1,0:T(8,128)(2,1)}), bf16[4,128,1536]{2,1,0:T(8,128)(2,1)}, u32[]{:S(2)}, u32[]{:S(2)}) async-start(bf16[4,128,1536]{2,1,0:T(8,128)(2,1)} %fusion), calls=%async_computation.4 | async-start | bytes 3145728 | tf_op jit(solution)/shard_map/all_to_all | solution.py:54
  289.7 5.8 %collective-permute-start.1 = (bf16[192,512]{0,1:T(8,128)(2,1)S(1)}, bf16[192,512]{0,1:T(8,128)(2,1)}, u32[]{:S(2)}, u32[]{:S(2)}) collective-permute-start(bf16[192,512]{0,1:T(8,128)(2,1)S(1)} %get-tuple-element.15), channel_id=1, source_target_pairs={{0,4},{4,0},{8,12},{12,8},{16,20},{20,16},{24,28},{28,24},{1,5},{5... | collective-permute-start | bytes 589832 | tf_op jit(solution)/shard_map/ppermute | solution.py:21
  289.8 18.2 %collective-permute-start.2 = (bf16[192,512]{0,1:T(8,128)(2,1)S(1)}, bf16[192,512]{0,1:T(8,128)(2,1)}, u32[]{:S(2)}, u32[]{:S(2)}) collective-permute-start(bf16[192,512]{0,1:T(8,128)(2,1)S(1)} %get-tuple-element.14), channel_id=1, source_target_pairs={{0,8},{4,12},{8,0},{12,4},{16,24},{20,28},{24,16},{28,20},{1,9},{5... | collective-permute-start | bytes 589832 | tf_op jit(solution)/shard_map/ppermute | solution.py:21
  289.9 28.7 %collective-permute-start.3 = (bf16[192,512]{0,1:T(8,128)(2,1)}, bf16[192,512]{0,1:T(8,128)(2,1)}, u32[]{:S(2)}, u32[]{:S(2)}) collective-permute-start(bf16[192,512]{0,1:T(8,128)(2,1)} %get-tuple-element.13), channel_id=1, source_target_pairs={{0,12},{4,8},{8,4},{12,0},{16,28},{20,24},{24,20},{28,16},{1,13},{... | collective-permute-start | bytes 589832 | tf_op jit(solution)/shard_map/ppermute | solution.py:21
  291.7 27.9 %collective-permute-start.4 = (bf16[192,512]{0,1:T(8,128)(2,1)}, bf16[192,512]{0,1:T(8,128)(2,1)}, u32[]{:S(2)}, u32[]{:S(2)}) collective-permute-start(bf16[192,512]{0,1:T(8,128)(2,1)} %get-tuple-element.12), channel_id=1, source_target_pairs={{0,16},{4,20},{8,24},{12,28},{16,0},{20,4},{24,8},{28,12},{1,17},{... | collective-permute-start | bytes 589832 | tf_op jit(solution)/shard_map/ppermute | solution.py:21
  292.9 31.2 %collective-permute-start.5 = (bf16[192,512]{0,1:T(8,128)(2,1)}, bf16[192,512]{0,1:T(8,128)(2,1)}, u32[]{:S(2)}, u32[]{:S(2)}) collective-permute-start(bf16[192,512]{0,1:T(8,128)(2,1)} %get-tuple-element.11), channel_id=1, source_target_pairs={{0,20},{4,16},{8,28},{12,24},{16,4},{20,0},{24,12},{28,8},{1,21},{... | collective-permute-start | bytes 589832 | tf_op jit(solution)/shard_map/ppermute | solution.py:21
  295.5 29.7 %collective-permute-start.6 = (bf16[192,512]{0,1:T(8,128)(2,1)}, bf16[192,512]{0,1:T(8,128)(2,1)}, u32[]{:S(2)}, u32[]{:S(2)}) collective-permute-start(bf16[192,512]{0,1:T(8,128)(2,1)} %get-tuple-element.10), channel_id=1, source_target_pairs={{0,24},{4,28},{8,16},{12,20},{16,8},{20,12},{24,0},{28,4},{1,25},{... | collective-permute-start | bytes 589832 | tf_op jit(solution)/shard_map/ppermute | solution.py:21
  308.0 18.2 %collective-permute-start.7 = (bf16[192,512]{0,1:T(8,128)(2,1)S(1)}, bf16[192,512]{0,1:T(8,128)(2,1)}, u32[]{:S(2)}, u32[]{:S(2)}) collective-permute-start(bf16[192,512]{0,1:T(8,128)(2,1)S(1)} %get-tuple-element.9), channel_id=1, source_target_pairs={{0,28},{4,24},{8,20},{12,16},{16,12},{20,8},{24,4},{28,0},{1,29},{... | collective-permute-start | bytes 589832 | tf_op jit(solution)/shard_map/ppermute | solution.py:21
  313.8 17.0 %all-to-all-start.5 = ((bf16[4,128,384]{2,1,0:T(8,128)(2,1)}), bf16[4,128,384]{2,1,0:T(8,128)(2,1)S(1)}, u32[]{:S(2)}, u32[]{:S(2)}) async-start(bf16[4,128,384]{2,1,0:T(8,128)(2,1)} %copy.110), calls=%async_computation.5 | async-start | bytes 786432 | tf_op jit(solution)/shard_map/all_to_all | solution.py:59
